TPU v7x, 256 devices: a whole 4x4x8 slice. The times are simulated.
256 devices in a mesh: dp: 32 (over z, y), tensor: 8 (over x, core).
Axes of the slice: x: 4, y: 4, z: 8, core: 2. Of those that a mesh axis runs over, the one named last changes fastest.
Arguments:
- out_grad: bfloat16 [8192, 4096], P('dp'), may hold values from -0.29882812 to 0.29882812
- hidden: bfloat16 [8192, 28672], P('dp', 'tensor'), may hold values from -60 to 60
- momentum: float32 [4096, 28672], P('dp', 'tensor'), may hold values from -48 to 48
- second: float32 [4096], P('dp'), may hold values from 0.01 to 0.2
Outputs:
- update: bfloat16 [4096, 28672], P('dp', 'tensor')
- momentum_out: float32 [4096, 28672], P('dp', 'tensor')
- second_out: float32 [4096], P('dp')
All inputs are finite; a program needn't handle non-finite values.
Results may differ from a plain program's by a relative error of at most 0.035.
Values may be sent and summed in bfloat16 or wider, within the bound.
No kernel may reach another device: no remote copies, remote signals or barrier semaphores. Data moves between devices by JAX's collectives and lax.ppermute only.
A program may use at most 128 MiB of HBM per device.

v0:
```python
import jax
import jax.numpy as jnp
from jax import lax
from jax.sharding import PartitionSpec as P

FF = 28672
ITERS = 3


quintic_a = 3.4445
quintic_b = -4.775
quintic_c = 2.0315
beta_one = 0.95
beta_two = 0.95


def sent_to_all(x, axis):
    count = lax.axis_size(axis)
    return lax.all_to_all(jnp.broadcast_to(x[None], (count, *x.shape)), axis, 0, 0, tiled=True)


def of_everyone(x, axis):
    everything = sent_to_all(x, axis)
    return jnp.sum(everything.astype(jnp.float32), axis=0)


def taken_together(x, axis):
    everything = sent_to_all(x, axis)
    return jnp.sum(everything, axis=0)


def summed_gram(partial_gram):
    return of_everyone(partial_gram.astype(jnp.bfloat16), "tensor").astype(jnp.float32)


def newton_schulz(current, reduce_gram):
    for iteration in range(ITERS):
        gram = reduce_gram(jnp.dot(current, current.T, preferred_element_type=jnp.float32)).astype(
            jnp.bfloat16
        )
        square = jnp.dot(gram, gram, preferred_element_type=jnp.float32)
        poly = (quintic_b * gram.astype(jnp.float32) + quintic_c * square).astype(jnp.bfloat16)
        current = (
            quintic_a * current.astype(jnp.float32)
            + jnp.dot(poly, current, preferred_element_type=jnp.float32)
        ).astype(jnp.bfloat16)
    return current


def body(out_grad, hidden, momentum, second):
    grad = lax.psum_scatter(
        lax.dot_general(
            out_grad, hidden, (((0,), (0,)), ((), ())), preferred_element_type=jnp.float32
        ).astype(jnp.bfloat16),
        "dp",
        scatter_dimension=0,
        tiled=True,
    ).astype(jnp.float32)
    momentum_out = beta_one * momentum + grad
    nesterov = grad + beta_one * momentum_out
    norm_sum = taken_together(jnp.sum(nesterov * nesterov), "tensor")
    start_panel = (nesterov / (jnp.sqrt(norm_sum) + 1e-07)).astype(jnp.bfloat16)
    orthogonal = newton_schulz(start_panel, summed_gram)
    local_wide = orthogonal.astype(jnp.float32)
    energy = taken_together(jnp.sum(local_wide * local_wide, axis=1), "tensor")
    second_out = beta_two * second + (1.0 - beta_two) * energy
    update = (orthogonal.astype(jnp.float32) * jnp.sqrt(FF / second_out)[:, None]).astype(
        jnp.bfloat16
    )
    return (update, momentum_out, second_out)


def solution(mesh):
    placed = (P("dp", None), P("dp", "tensor"), P("dp", "tensor"), P("dp"))
    return jax.shard_map(
        body,
        mesh=mesh,
        in_specs=placed,
        out_specs=(P("dp", "tensor"), P("dp", "tensor"), P("dp")),
        check_vma=False,
    )
```

profile of v0, /device:TPU:1, one launch (start us, length us, event | category | flops | bytes accessed | tf_op | source)
XLA Modules:
  0.0 386.0 jit_solution(8228609359193561105)
XLA Ops:
  7.2 0.0 copy-start
  7.2 0.0 reduce-scatter.2.cloned.1.call-start
  7.2 1.5 copy-done
  8.8 13.9 %convolution_convert_fusion = bf16[4096,3584]{1,0:T(8,128)(2,1)} fusion(bf16[256,4096]{1,0:T(8,128)(2,1)S(1)} %copy-done, bf16[256,3584]{1,0:T(8,128)(2,1)} %param.5), kind=kOutput, calls=%fused_computation | convolution fusion | flops 7530872832 | bytes 33292288 | tf_op jit(solution)/shard_map/dot_general | solution.py:52
  22.7 0.0 reduce-scatter.2.cloned.1.call-update
  22.7 290.1 %reduce-scatter.2.cloned.1.call-done = bf16[128,3584]{1,0:T(8,128)(2,1)} async-done(((bf16[4096,3584]{1,0:T(8,128)(2,1)}), bf16[128,3584]{1,0:T(8,128)(2,1)}) %reduce-scatter.2.cloned.1.call-update) | async-done | bytes 917520 | tf_op jit(solution)/shard_map/reduce_scatter | solution.py:51
  312.8 4.1 %multiply_reduce_fusion.1 = (f32[]{:T(128)}, f32[128,3584]{1,0:T(8,128)}) fusion(bf16[128,3584]{1,0:T(8,128)(2,1)} %reduce-scatter.2.cloned.1.call-done, f32[128,3584]{1,0:T(8,128)} %param.6), kind=kLoop, calls=%fused_computation.13 | loop fusion | flops 3211263 | bytes 4587524 | tf_op jit(solution)/shard_map/reduce_sum | solution.py:61
  316.9 0.6 broadcast_in_dim.10
  317.6 9.7 %all_to_all.27 = f32[8,1,1]{2,1,0:T(1,128)S(1)} all-to-all(f32[8,1,1]{2,1,0:T(1,128)S(1)} %broadcast_in_dim.10), channel_id=1, replica_groups=mesh['dp'=32,'tensor'=8] {'tensor'}, dimensions={0} | all-to-all | bytes 64 | tf_op jit(solution)/shard_map/all_to_all | solution.py:19
  327.3 0.6 reduce_sum.73
  328.6 1.8 divide_convert_fusion
  330.4 0.9 copy-done.2
  331.3 0.4 convolution_convert_fusion.3
  331.7 9.6 %all_to_all.28 = bf16[8,128,128]{2,1,0:T(8,128)(2,1)S(1)} all-to-all(bf16[8,128,128]{2,1,0:T(8,128)(2,1)S(1)} %broadcast_in_dim.11), channel_id=1, replica_groups=mesh['dp'=32,'tensor'=8] {'tensor'}, dimensions={0} | all-to-all | bytes 524288 | tf_op jit(solution)/shard_map/all_to_all | solution.py:19
  341.4 2.0 fusion
  343.4 0.4 convolution_convert_fusion.2
  343.9 9.9 %all_to_all.29 = bf16[8,128,128]{2,1,0:T(8,128)(2,1)S(1)} all-to-all(bf16[8,128,128]{2,1,0:T(8,128)(2,1)S(1)} %broadcast_in_dim.12), channel_id=1, replica_groups=mesh['dp'=32,'tensor'=8] {'tensor'}, dimensions={0} | all-to-all | bytes 524288 | tf_op jit(solution)/shard_map/all_to_all | solution.py:19
  353.8 2.0 fusion.1
  355.9 0.4 convolution_convert_fusion.1
  356.3 9.9 %all_to_all.30 = bf16[8,128,128]{2,1,0:T(8,128)(2,1)S(1)} all-to-all(bf16[8,128,128]{2,1,0:T(8,128)(2,1)S(1)} %broadcast_in_dim.13), channel_id=1, replica_groups=mesh['dp'=32,'tensor'=8] {'tensor'}, dimensions={0} | all-to-all | bytes 524288 | tf_op jit(solution)/shard_map/all_to_all | solution.py:19
  366.3 1.8 multiply_reduce_fusion
  368.1 8.0 %all_to_all.31 = f32[8,1,128]{2,1,0:T(1,128)S(1)} all-to-all(f32[8,1,128]{2,1,0:T(1,128)S(1)} %broadcast_in_dim.14), channel_id=1, replica_groups=mesh['dp'=32,'tensor'=8] {'tensor'}, dimensions={0} | all-to-all | bytes 8192 | tf_op jit(solution)/shard_map/all_to_all | solution.py:19
  376.1 0.5 divide_sqrt_fusion
  376.6 2.6 multiply_convert_fusion
  (15 shorter events, 0.3 us)
Async XLA Ops:
  7.2 1.6 copy-start
  7.2 305.6 %reduce-scatter.2.cloned.1.call-start = ((), (), s32[]{:S(2)}) async-start(), calls=%async_computation.6 | async-start | bytes 30277632 | tf_op jit(solution)/shard_map/reduce_scatter | solution.py:51
  312.8 15.8 %copy-start.3 = (bf16[128,3584]{1,0:T(8,128)(2,1)S(1)}, bf16[128,3584]{1,0:T(8,128)(2,1)}, u32[]{:S(2)}) copy-start(bf16[128,3584]{1,0:T(8,128)(2,1)} %reduce-scatter.2.cloned.1.call-done) | copy-start | bytes 2752516
  330.4 0.9 copy-start.2
  343.4 10.4 %copy-start.1 = (bf16[128,3584]{1,0:T(8,128)(2,1)}, bf16[128,3584]{1,0:T(8,128)(2,1)S(1)}, u32[]{:S(2)}) copy-start(bf16[128,3584]{1,0:T(8,128)(2,1)S(1)} %fusion) | copy-start | bytes 2752516
  356.3 19.8 %copy-start.4 = (f32[128]{0:T(128)S(1)}, f32[128]{0:T(128)}, u32[]{:S(2)}) copy-start(f32[128]{0:T(128)} %param.7) | copy-start | bytes 1540
Sparse Core Ops, SparseCore 0:
  22.8 289.9 reduce-scatter.1
where the time goes:
time: 386 us
  waiting for transfers between devices  290 us (75%)
  blocking collectives  47.2 us (12%)
  matrix products  20.9 us (5%)
  between operations  14.8 us (4%)
  other arithmetic  9.71 us (3%)
    reduce_scatter x1, waiting for transfers between devices, body(): lax.psum_scatter(lax.dot_general(out_grad, hidden, (((0,), (0,)), ((), ()...  290 us
    all_to_all x5, blocking collectives, sent_to_all(): lax.all_to_all(jnp.broadcast_to(x[None], (count, *x.shape)), axis, 0, 0,...  47.2 us
    dot_general x1, matrix products, body(): lax.dot_general(out_grad, hidden, (((0,), (0,)), ((), ())), preferred_ele...  13.9 us
  transfers between devices with their start and end apart: 1, of which 1 were waited for; matrix products, arithmetic and copies ran while one was open for 0% of the time, Pallas kernels for 0%

commit v1 on v0

v1 whole, which is shorter than its diff:
```python
import jax
import jax.numpy as jnp
from jax import lax
from jax.experimental import pallas as pl
from jax.experimental.pallas import tpu as pltpu
from jax.sharding import Mesh, PartitionSpec as P

FF = 28672
ITERS = 3
quintic_a = 3.4445
quintic_b = -4.775
quintic_c = 2.0315
beta_one = 0.95
beta_two = 0.95
NZ, NY, NX, NC = 8, 4, 4, 2
SIZES = {"z": NZ, "y": NY, "x": NX, "core": NC}
TENSOR = ("x", "core")
CHUNKS = (1024, 1280, 1280)
TILE = 256
ORDER = (
    "v0 n0 n1 w0", "f0 n2 f1 x0", "T0 o0 P0 a0", "b0 o1 P1 f2", "a1 c0 b1 d0", "c1 o2 P2 a2",
    "d1 b2 c2 d2",
)
DEPTH = 4
AHEAD = {"f2": 0}
INSTEAD = {}
PANEL = 128
TOKENS = 256
SHARE = TOKENS // (NX * NC)
DISTANCES = (3, 2, 1, 0, 4)
VMEM = pl.BlockSpec(memory_space=pltpu.VMEM)
SMEM = pl.BlockSpec(memory_space=pltpu.SMEM)
LIMIT = pltpu.CompilerParams(vmem_limit_bytes=40 << 20)


def shifted(x, axis, by):
    count = SIZES[axis]
    return lax.ppermute(x, axis, [(i, (i + by) % count) for i in range(count)])


def core_swapped(x):
    return lax.ppermute(x, "core", [(0, 1), (1, 0)])


def around(x, axis):
    count = SIZES[axis]
    pairs = [(2 * i + c, 2 * ((i + 1 - 2 * c) % count) + c) for i in range(count) for c in range(2)]
    return lax.ppermute(x, (axis, "core"), pairs)


def after(x, *others):
    return lax.optimization_barrier((x,) + others)[0]


def shape(*dims, dtype=jnp.bfloat16):
    return jax.ShapeDtypeStruct(dims, dtype)


def source_kernel(place, out_grad, above, below, across):
    y = place[1]
    for by, out in ((1, above), (NY - 1, below), (2, across)):
        target = lax.rem(y + by, NY)
        for z in range(NZ):
            lane = pl.multiple_of((z * NY + target) * PANEL, PANEL)
            out[:, z * PANEL:(z + 1) * PANEL] = out_grad[:, pl.ds(lane, PANEL)]


def source(place, out_grad):
    whole = pl.BlockSpec((SHARE, NZ * PANEL), lambda i, place: (0, 0))
    return pl.pallas_call(
        source_kernel,
        grid_spec=pltpu.PrefetchScalarGridSpec(
            num_scalar_prefetch=1,
            grid=(1,),
            in_specs=[pl.BlockSpec((SHARE, NZ * NY * PANEL), lambda i, place: (place[4], 0))],
            out_specs=[whole] * 3,
        ),
        out_shape=[shape(SHARE, NZ * PANEL)] * 3,
        name="source",
    )(place, out_grad)


def turn_kernel(place, out_grad, both, near, far, other, turned, spread):
    z, y, c, x = place[0], place[1], place[2], place[3]
    step = 1 - 2 * c
    shares = (
        (0, c, lambda k: both[0, k]), (0, 1 - c, lambda k: both[1, k]),
        (NX - step, c, lambda k: near[0, k]), (NX - step, 1 - c, lambda k: near[1, k]),
        (NX + step, c, lambda k: other[1, k]), (NX + step, 1 - c, lambda k: other[0, k]),
        (2, c, lambda k: far[k]), (2, 1 - c, lambda k: other[2, k]),
    )
    for chip, core, piece in shares:
        at = pl.multiple_of((lax.rem(x + chip, NX) * NC + core) * SHARE, SHARE)
        for k in range(NY - 1):
            spread[k, pl.ds(at, SHARE)] = piece(k)
    for i, distance in enumerate(DISTANCES):
        owner = lax.rem(z + step * distance + NZ, NZ)
        lane = pl.multiple_of((owner * NY + y) * PANEL, PANEL)
        rows = slice(i * PANEL, (i + 1) * PANEL)
        turned[rows, 0:TOKENS] = out_grad[:, pl.ds(lane, PANEL)].T
        lane = pl.multiple_of(owner * PANEL, PANEL)
        for k, of in enumerate((c, 1 - c, 2)):
            turned[rows, (k + 1) * TOKENS:(k + 2) * TOKENS] = spread[of, :, pl.ds(lane, PANEL)].T


def turned_cotangent(place, out_grad, *others):
    return pl.pallas_call(
        turn_kernel,
        in_specs=[SMEM] + [VMEM] * 5,
        out_specs=VMEM,
        out_shape=shape(len(DISTANCES) * PANEL, NY * TOKENS),
        scratch_shapes=[pltpu.VMEM((NY - 1, TOKENS, NZ * PANEL), jnp.bfloat16)],
        compiler_params=LIMIT,
        cost_estimate=pl.CostEstimate(flops=0, bytes_accessed=6 << 20, transcendentals=0),
        name="turn",
    )(place, out_grad, *others)


def product_kernel(turned, part, sibling, near, far, other, three, two, one, own, four):
    width = part.shape[1]

    def summed(rows, blocks):
        return jnp.dot(
            turned[0:rows], jnp.concatenate(blocks, axis=0), preferred_element_type=jnp.float32
        ).astype(jnp.bfloat16)

    @pl.loop(0, width // TILE)
    def _(j):
        at = pl.ds(pl.multiple_of(j * TILE, TILE), TILE)
        mine = summed(5 * PANEL, [part[:, at], near[0, :, at], other[1, :, at], far[:, at]])
        for i, out in enumerate((three, two, one)):
            out[0, :, at] = mine[i * PANEL:(i + 1) * PANEL]
        own[:, at] = mine[3 * PANEL:4 * PANEL]
        four[:, at] = mine[4 * PANEL:]
        theirs = summed(3 * PANEL, [sibling[:, at], near[1, :, at], other[0, :, at], other[2, :, at]])
        for i, out in enumerate((three, two, one)):
            out[1, :, at] = theirs[i * PANEL:(i + 1) * PANEL]


def product(turned, parts):
    width = parts[0].shape[1]
    flops = 2 * NY * TOKENS * NZ * PANEL * width
    return pl.pallas_call(
        product_kernel,
        in_specs=[VMEM] * 6,
        out_specs=[VMEM] * 5,
        out_shape=[shape(2, PANEL, width)] * 3 + [shape(PANEL, width)] * 2,
        compiler_params=LIMIT,
        cost_estimate=pl.CostEstimate(flops=flops, bytes_accessed=6 * TOKENS * width * 2, transcendentals=0),
        name="product",
    )(turned, *parts)


def added(x, y):
    return (x.astype(jnp.float32) + y.astype(jnp.float32)).astype(jnp.bfloat16)


def blend_kernel(*refs):
    n = len(CHUNKS)
    pieces, momentum, (momentum_out, panel, grams) = refs[:3 * n], refs[3 * n], refs[3 * n + 1:]
    gram, start = None, 0
    for i, width in enumerate(CHUNKS):
        own, ring, swapped = pieces[3 * i:3 * i + 3]
        at = slice(start, start + width)
        grad = own[...].astype(jnp.float32) + ring[0].astype(jnp.float32) + swapped[...].astype(jnp.float32)
        new = beta_one * momentum[:, at] + grad
        momentum_out[:, at] = new
        p = (grad + beta_one * new).astype(jnp.bfloat16)
        panel[:, at] = p
        g = lax.dot_general(p, p, (((1,), (1,)), ((), ())), preferred_element_type=jnp.float32)
        gram = g if gram is None else gram + g
        start += width
    gram = gram.astype(jnp.bfloat16)
    for i in range(NX * NC):
        grams[i] = gram


def blended(pieces, momentum):
    rows, columns = momentum.shape
    return pl.pallas_call(
        blend_kernel,
        in_specs=[VMEM] * (len(pieces) + 1),
        out_specs=[VMEM] * 3,
        out_shape=[shape(rows, columns, dtype=jnp.float32), shape(rows, columns), shape(NX * NC, rows, rows)],
        compiler_params=LIMIT,
        name="blend",
    )(*pieces, momentum)


def finish_kernel(grams, second, panel, update, second_out):
    def mul(a, b):
        return jnp.dot(a, b, precision=lax.Precision.HIGHEST, preferred_element_type=jnp.float32)

    raw = jnp.sum(grams[...].astype(jnp.float32), axis=0)
    eye = lax.broadcasted_iota(jnp.int32, (PANEL, PANEL), 0) == lax.broadcasted_iota(jnp.int32, (PANEL, PANEL), 1)
    norm = jnp.sqrt(jnp.sum(jnp.where(eye, raw, 0.0), keepdims=True))
    scale = 1.0 / (norm + 1e-07)
    gram = raw * scale * scale
    unit = jnp.where(eye, quintic_a, 0.0)
    total = None
    for _ in range(ITERS):
        factor = unit + quintic_b * gram + quintic_c * mul(gram, gram)
        total = factor if total is None else mul(factor, total)
        gram = mul(mul(factor, gram), factor)
    energy = jnp.sum(jnp.where(eye, gram, 0.0), axis=0, keepdims=True)
    new = beta_two * second[...] + (1.0 - beta_two) * energy
    second_out[...] = new
    row = jnp.sum(jnp.where(eye, jnp.sqrt(FF / new), 0.0), axis=1, keepdims=True)
    total = total * scale
    high = total.astype(jnp.bfloat16)
    low = (total - high.astype(jnp.float32)).astype(jnp.bfloat16)
    for start in range(0, panel.shape[1], 512):
        p = panel[:, start:start + 512]
        x = jnp.dot(high, p, preferred_element_type=jnp.float32) + jnp.dot(low, p, preferred_element_type=jnp.float32)
        x = x.astype(jnp.bfloat16).astype(jnp.float32)
        update[:, start:start + 512] = (x * row).astype(jnp.bfloat16)


def finished(grams, second, panel):
    update, second_out = pl.pallas_call(
        finish_kernel,
        in_specs=[VMEM] * 3,
        out_specs=[VMEM] * 2,
        out_shape=[shape(*panel.shape), shape(1, PANEL, dtype=jnp.float32)],
        compiler_params=LIMIT,
        name="finish",
    )(grams, second[None], panel)
    return update, second_out[0]


def body(out_grad, hidden, momentum, second):
    z, y, x, core = [lax.axis_index(name) for name in ("z", "y", "x", "core")]
    place = jnp.stack([z, y, core, x, x * NC + core]).astype(jnp.int32)
    n = len(CHUNKS)
    starts = [sum(CHUNKS[:i]) for i in range(n)]
    part = [hidden[:, i:i + width] for i, width in zip(starts, CHUNKS)]
    sibling, near, far, other, made, ring = [[None] * n for _ in range(6)]
    got = jnp.stack([shifted(a, "y", by) for a, by in zip(source(place, out_grad), (1, -1, 2))])
    both = jnp.stack([got, core_swapped(got)])
    for i in range(n):
        sibling[i] = core_swapped(after(part[i], sibling[i - 1]) if i else part[i])
    arrived = [got]

    named = {}

    def sent(send, x, *args):
        x = after(x, named[INSTEAD[act]] if act in INSTEAD else arrived[max(0, len(arrived) - DEPTH)])
        if act in AHEAD:
            x = after(x, made[AHEAD[act]][4])
        arrived.append(send(x, *args))
        named[act] = arrived[-1]
        return arrived[-1]

    def joined(near, far):
        return jnp.concatenate([near, far[None]], axis=0)

    for act in " ".join(ORDER).split():
        kind, i = act[0], int(act[1])
        if kind == "v":
            near_a = sent(around, both, "x")
        elif kind == "w":
            far_a = sent(around, near_a[0], "x")
        elif kind == "x":
            other_a = core_swapped(joined(near_a, far_a))
        elif kind == "T":
            turned = turned_cotangent(place, out_grad, both, near_a, far_a, other_a)
        elif kind == "n":
            near[i] = sent(around, jnp.stack([part[i], sibling[i]]), "y")
        elif kind == "f":
            far[i] = sent(around, near[i][0], "y")
        elif kind == "o":
            other[i] = core_swapped(joined(near[i], far[i]))
        elif kind == "P":
            made[i] = product(turned, (part[i], sibling[i], near[i], far[i], other[i]))
        elif kind == "a":
            ring[i] = sent(around, made[i][4], "z")
        elif kind == "b":
            three = made[i][0]
            ring[i] = sent(around, jnp.stack([added(ring[i], three[0]), three[1]]), "z")
        elif kind in "cd":
            ring[i] = sent(around, added(ring[i], made[i]["cd".index(kind) + 1]), "z")
    pieces = [x for i in range(n) for x in (made[i][3], ring[i], core_swapped(ring[i][1]))]
    momentum_out, panel, grams = blended(pieces, momentum)
    grams = lax.all_to_all(grams, TENSOR, 0, 0, tiled=True)
    update, second_out = finished(grams, second, panel)
    return update, momentum_out, second_out


def solution(mesh):
    cube = Mesh(mesh.devices.reshape(NZ, NY, NX, NC), ("z", "y", "x", "core"))
    dp = ("z", "y")
    placed = (P(dp, None), P(dp, TENSOR), P(dp, TENSOR), P(dp))
    return jax.shard_map(
        body,
        mesh=cube,
        in_specs=placed,
        out_specs=(P(dp, TENSOR), P(dp, TENSOR), P(dp)),
        check_vma=False,
    )
```

time: 386 us -> 184 us (0.48)
  waiting for transfers between devices: 290 us -> 79 us
  starting transfers between devices: 0.04 us -> 69.5 us
  blocking collectives: 47.2 us -> 10.9 us
  matrix products: 20.9 us -> 0 us
  Pallas kernels: 0 us -> 19 us
  between operations: 14.8 us -> 0.95 us
  other arithmetic: 9.71 us -> 2.33 us
    reduce_scatter x1 -> x0, waiting for transfers between devices: 290 us -> none  [body(): lax.psum_scatter(lax.dot_general(out_grad, hidden, (((0,), (0,)), ((), ()...]
    ppermute x0 -> x34, waiting for transfers between devices: none -> 79 us  [the longest x20 70.7 us: around(): return lax.ppermute(x, (axis, 'core'), pairs)]
    ppermute x0 -> x34, starting transfers between devices: none -> 69.5 us  [the longest x20 37.3 us: around(): return lax.ppermute(x, (axis, 'core'), pairs)]
    all_to_all x5 -> x1, blocking collectives: 47.2 us -> 10.9 us  [body(): grams = lax.all_to_all(grams, TENSOR, 0, 0, tiled=True)]
    dot_general x7 -> x0, matrix products: 20.9 us -> none  [the longest x1 13.9 us: body(): lax.dot_general(out_grad, hidden, (((0,), (0,)), ((), ())), preferred_ele...]
    pallas_call x0 -> x7, Pallas kernels: none -> 19 us  [the longest x3 10.1 us: product(): pl.pallas_call(product_kernel, in_specs=[VMEM] * 6, out_specs=[VMEM] * 5,...]
    reduce_sum x6 -> x0, other arithmetic: 4.83 us -> none  [the longest x1 4.09 us: body(): norm_sum = taken_together(jnp.sum(nesterov * nesterov), 'tensor')]
  transfers between devices with their start and end apart: 1 -> 34, of which waited for: 1 -> 19; matrix products, arithmetic and copies ran while one was open for 0% -> 2% of each run, Pallas kernels for 0% -> 7%
where the time goes in v1:
time: 184 us
  waiting for transfers between devices  79 us (43%)
  starting transfers between devices  69.5 us (38%)
  Pallas kernels  19 us (10%)
  blocking collectives  10.9 us (6%)
  other arithmetic  2.33 us (1%)
  local copies, waits for them, and re-layouts  2.23 us (1%)
    ppermute x20, waiting for transfers between devices, around(): return lax.ppermute(x, (axis, 'core'), pairs)  70.7 us
    ppermute x20, starting transfers between devices, around(): return lax.ppermute(x, (axis, 'core'), pairs)  37.3 us
    ppermute x11, starting transfers between devices, core_swapped(): return lax.ppermute(x, 'core', [(0, 1), (1, 0)])  29.5 us
    all_to_all x1, blocking collectives, body(): grams = lax.all_to_all(grams, TENSOR, 0, 0, tiled=True)  10.9 us
    pallas_call x3, Pallas kernels, product(): pl.pallas_call(product_kernel, in_specs=[VMEM] * 6, out_specs=[VMEM] * 5,...  10.1 us
    ppermute x3, waiting for transfers between devices, shifted(): return lax.ppermute(x, axis, [(i, (i + by) % count) for i in range(count)])  4.83 us
  transfers between devices with their start and end apart: 34, of which 19 were waited for; matrix products, arithmetic and copies ran while one was open for 2% of the time, Pallas kernels for 7%

profile of v1, /device:TPU:1, one launch (start us, length us, event | category | flops | bytes accessed | tf_op | source)
XLA Modules:
  0.0 183.9 jit_solution(500828364111029008)
XLA Ops:
  1.8 3.3 %collective-permute-start.7 = (bf16[256,1024]{1,0:T(8,128)(2,1)S(1)}, bf16[256,1024]{1,0:T(8,128)(2,1)S(1)}, u32[]{:S(2)}, u32[]{:S(2)}) collective-permute-start(bf16[256,1024]{1,0:T(8,128)(2,1)S(1)} %get-tuple-element.100.part), channel_id=1, source_target_pairs={{0,1},{1,0},{2,3},{3,2},{4,5},{5,4},{6,7},{7,6},{8,9},{9,8},{10,11... | collective-permute-start | bytes 1572872 | tf_op jit(solution)/shard_map/ppermute | solution.py:42
  23.8 5.9 %collective-permute-done.8.near = bf16[2,256,1024]{2,1,0:T(8,128)(2,1)S(1)} collective-permute-done((bf16[2,256,1024]{2,1,0:T(8,128)(2,1)S(1)}, bf16[2,256,1024]{2,1,0:T(8,128)(2,1)S(1)}, u32[]{:S(2)}, u32[]{:S(2)}) %collective-permute-start.8) | collective-permute-done | bytes 1048608 | tf_op jit(solution)/shard_map/ppermute | solution.py:48
  33.4 4.1 %collective-permute-done.5.far = bf16[3,32,1024]{2,1,0:T(8,128)(2,1)S(1)} collective-permute-done((bf16[3,32,1024]{2,1,0:T(8,128)(2,1)S(1)}, bf16[3,32,1024]{2,1,0:T(8,128)(2,1)S(1)}, u32[]{:S(2)}, u32[]{:S(2)}) %collective-permute-start.5) | collective-permute-done | bytes 196640 | tf_op jit(solution)/shard_map/ppermute | solution.py:48
  37.5 3.3 %collective-permute-start.6 = (bf16[3,3,32,1024]{3,2,1,0:T(8,128)(2,1)S(1)}, bf16[3,3,32,1024]{3,2,1,0:T(8,128)(2,1)S(1)}, u32[]{:S(2)}, u32[]{:S(2)}) collective-permute-start(bf16[3,3,32,1024]{3,2,1,0:T(8,128)(2,1)S(1)} %pad_maximum_fusion.8), channel_id=1, source_target_pairs={{0,1},{1,0},{2,3},{3,2},{4,5},{5,4},{6,7},{7,6},{8,9},{9,8},{10,11... | collective-permute-start | bytes 1769480 | tf_op jit(solution)/shard_map/ppermute | solution.py:42
  40.8 8.6 %collective-permute-done.9.far = bf16[256,1024]{1,0:T(8,128)(2,1)S(1)} collective-permute-done((bf16[256,1024]{1,0:T(8,128)(2,1)S(1)}, bf16[256,1024]{1,0:T(8,128)(2,1)S(1)}, u32[]{:S(2)}, u32[]{:S(2)}) %collective-permute-start.9) | collective-permute-done | bytes 524320 | tf_op jit(solution)/shard_map/ppermute | solution.py:48
  49.5 3.9 %collective-permute-start.10 = (bf16[3,256,1024]{2,1,0:T(8,128)(2,1)S(1)}, bf16[3,256,1024]{2,1,0:T(8,128)(2,1)S(1)}, u32[]{:S(2)}, u32[]{:S(2)}) collective-permute-start(bf16[3,256,1024]{2,1,0:T(8,128)(2,1)S(1)} %pad_maximum_fusion.2), channel_id=1, source_target_pairs={{0,1},{1,0},{2,3},{3,2},{4,5},{5,4},{6,7},{7,6},{8,9},{9,8},{10,11... | collective-permute-start | bytes 4718600 | tf_op jit(solution)/shard_map/ppermute | solution.py:42
  55.0 8.4 %collective-permute-done.16.near = bf16[2,256,1280]{2,1,0:T(8,128)(2,1)S(1)} collective-permute-done((bf16[2,256,1280]{2,1,0:T(8,128)(2,1)S(1)}, bf16[2,256,1280]{2,1,0:T(8,128)(2,1)S(1)}, u32[]{:S(2)}, u32[]{:S(2)}) %collective-permute-start.16) | collective-permute-done | bytes 1310752 | tf_op jit(solution)/shard_map/ppermute | solution.py:48
  70.6 3.9 %collective-permute-start.22 = (bf16[3,256,1280]{2,1,0:T(8,128)(2,1)S(1)}, bf16[3,256,1280]{2,1,0:T(8,128)(2,1)S(1)}, u32[]{:S(2)}, u32[]{:S(2)}) collective-permute-start(bf16[3,256,1280]{2,1,0:T(8,128)(2,1)S(1)} %pad_maximum_fusion), channel_id=1, source_target_pairs={{0,1},{1,0},{2,3},{3,2},{4,5},{5,4},{6,7},{7,6},{8,9},{9,8},{10,11... | collective-permute-start | bytes 5898248 | tf_op jit(solution)/shard_map/ppermute | solution.py:42
  74.5 3.8 %collective-permute-start.11 = (bf16[128,1024]{1,0:T(8,128)(2,1)S(1)}, bf16[128,1024]{1,0:T(8,128)(2,1)S(1)}, u32[]{:S(2)}, u32[]{:S(2)}) collective-permute-start(bf16[128,1024]{1,0:T(8,128)(2,1)S(1)} %get-tuple-element.58), channel_id=1, source_target_pairs={{0,32},{1,225},{32,64},{33,1},{64,96},{65,33},{96,128},{97,65},{12... | collective-permute-start | bytes 786440 | tf_op jit(solution)/shard_map/ppermute | solution.py:48
  78.5 3.8 %collective-permute-start.28 = (bf16[3,256,1280]{2,1,0:T(8,128)(2,1)S(1)}, bf16[3,256,1280]{2,1,0:T(8,128)(2,1)S(1)}, u32[]{:S(2)}, u32[]{:S(2)}) collective-permute-start(bf16[3,256,1280]{2,1,0:T(8,128)(2,1)S(1)} %pad_maximum_fusion.1), channel_id=1, source_target_pairs={{0,1},{1,0},{2,3},{3,2},{4,5},{5,4},{6,7},{7,6},{8,9},{9,8},{10,11... | collective-permute-start | bytes 5898248 | tf_op jit(solution)/shard_map/ppermute | solution.py:42
  82.5 3.9 %collective-permute-start.12 = (bf16[2,128,1024]{2,1,0:T(8,128)(2,1)S(1)}, bf16[2,128,1024]{2,1,0:T(8,128)(2,1)S(1)}, u32[]{:S(2)}, u32[]{:S(2)}) collective-permute-start(bf16[2,128,1024]{2,1,0:T(8,128)(2,1)S(1)} %pad_maximum_fusion.9), channel_id=1, source_target_pairs={{0,32},{1,225},{32,64},{33,1},{64,96},{65,33},{96,128},{97,65},{12... | collective-permute-start | bytes 1572872 | tf_op jit(solution)/shard_map/ppermute | solution.py:48
  86.4 6.1 %collective-permute-done.12 = bf16[2,128,1024]{2,1,0:T(8,128)(2,1)S(1)} collective-permute-done((bf16[2,128,1024]{2,1,0:T(8,128)(2,1)S(1)}, bf16[2,128,1024]{2,1,0:T(8,128)(2,1)S(1)}, u32[]{:S(2)}, u32[]{:S(2)}) %collective-permute-start.12) | collective-permute-done | bytes 524320 | tf_op jit(solution)/shard_map/ppermute | solution.py:48
  95.9 3.6 %product.4 = (bf16[2,128,1280]{2,1,0:T(8,128)(2,1)S(1)}, bf16[2,128,1280]{2,1,0:T(8,128)(2,1)S(1)}, bf16[2,128,1280]{2,1,0:T(8,128)(2,1)S(1)}, bf16[128,1280]{1,0:T(8,128)(2,1)S(1)}, bf16[128,1280]{1,0:T(8,128)(2,1)S(1)}) custom-call(bf16[640,1024]{1,0:T(8,128)(2,1)S(1)} %turn.1.turned, bf16[256,1280]{1,0:T(8,128)(2,1)S(1)} %get-tuple-element.64.part, ...), custom_call_target="tpu_custom_call" | custom-call | flops 2684354560 | bytes 3932160 | tf_op jit(solution)/shard_map/product/pallas_call | solution.py:143
  105.5 3.6 %product.5 = (bf16[2,128,1280]{2,1,0:T(8,128)(2,1)S(1)}, bf16[2,128,1280]{2,1,0:T(8,128)(2,1)S(1)}, bf16[2,128,1280]{2,1,0:T(8,128)(2,1)S(1)}, bf16[128,1280]{1,0:T(8,128)(2,1)S(1)}, bf16[128,1280]{1,0:T(8,128)(2,1)S(1)}) custom-call(bf16[640,1024]{1,0:T(8,128)(2,1)S(1)} %turn.1.turned, bf16[256,1280]{1,0:T(8,128)(2,1)S(1)} %get-tuple-element.65.part, ...), custom_call_target="tpu_custom_call" | custom-call | flops 2684354560 | bytes 3932160 | tf_op jit(solution)/shard_map/product/pallas_call | solution.py:143
  109.5 5.9 %collective-permute-done.29 = bf16[128,1280]{1,0:T(8,128)(2,1)S(1)} collective-permute-done((bf16[128,1280]{1,0:T(8,128)(2,1)S(1)}, bf16[128,1280]{1,0:T(8,128)(2,1)S(1)}, u32[]{:S(2)}, u32[]{:S(2)}) %collective-permute-start.29) | collective-permute-done | bytes 327712 | tf_op jit(solution)/shard_map/ppermute | solution.py:48
  118.5 4.0 %collective-permute-done.24 = bf16[2,128,1280]{2,1,0:T(8,128)(2,1)S(1)} collective-permute-done((bf16[2,128,1280]{2,1,0:T(8,128)(2,1)S(1)}, bf16[2,128,1280]{2,1,0:T(8,128)(2,1)S(1)}, u32[]{:S(2)}, u32[]{:S(2)}) %collective-permute-start.24) | collective-permute-done | bytes 655392 | tf_op jit(solution)/shard_map/ppermute | solution.py:48
  125.5 4.0 %collective-permute-done.30 = bf16[2,128,1280]{2,1,0:T(8,128)(2,1)S(1)} collective-permute-done((bf16[2,128,1280]{2,1,0:T(8,128)(2,1)S(1)}, bf16[2,128,1280]{2,1,0:T(8,128)(2,1)S(1)}, u32[]{:S(2)}, u32[]{:S(2)}) %collective-permute-start.30) | collective-permute-done | bytes 655392 | tf_op jit(solution)/shard_map/ppermute | solution.py:48
  129.6 6.9 %collective-permute-done.25 = bf16[2,128,1280]{2,1,0:T(8,128)(2,1)S(1)} collective-permute-done((bf16[2,128,1280]{2,1,0:T(8,128)(2,1)S(1)}, bf16[2,128,1280]{2,1,0:T(8,128)(2,1)S(1)}, u32[]{:S(2)}, u32[]{:S(2)}) %collective-permute-start.25) | collective-permute-done | bytes 655392 | tf_op jit(solution)/shard_map/ppermute | solution.py:48
  139.5 7.3 %collective-permute-done.31 = bf16[2,128,1280]{2,1,0:T(8,128)(2,1)S(1)} collective-permute-done((bf16[2,128,1280]{2,1,0:T(8,128)(2,1)S(1)}, bf16[2,128,1280]{2,1,0:T(8,128)(2,1)S(1)}, u32[]{:S(2)}, u32[]{:S(2)}) %collective-permute-start.31) | collective-permute-done | bytes 655392 | tf_op jit(solution)/shard_map/ppermute | solution.py:48
  150.2 3.7 %collective-permute-done.26.refs_4_ = bf16[2,128,1280]{2,1,0:T(8,128)(2,1)S(1)} collective-permute-done((bf16[2,128,1280]{2,1,0:T(8,128)(2,1)S(1)}, bf16[2,128,1280]{2,1,0:T(8,128)(2,1)S(1)}, u32[]{:S(2)}, u32[]{:S(2)}) %collective-permute-start.26) | collective-permute-done | bytes 655392 | tf_op jit(solution)/shard_map/ppermute | solution.py:48
  153.9 4.9 %collective-permute-start.27 = (bf16[128,1280]{1,0:T(8,128)(2,1)S(1)}, bf16[128,1280]{1,0:T(8,128)(2,1)S(1)}, u32[]{:S(2)}, u32[]{:S(2)}) collective-permute-start(bf16[128,1280]{1,0:T(8,128)(2,1)S(1)} %slice_bitcast_fusion.4), channel_id=1, source_target_pairs={{0,1},{1,0},{2,3},{3,2},{4,5},{5,4},{6,7},{7,6},{8,9},{9,8},{10,11... | collective-permute-start | bytes 983048 | tf_op jit(solution)/shard_map/ppermute | solution.py:42
  160.9 4.9 %collective-permute-start.33 = (bf16[128,1280]{1,0:T(8,128)(2,1)S(1)}, bf16[128,1280]{1,0:T(8,128)(2,1)S(1)}, u32[]{:S(2)}, u32[]{:S(2)}) collective-permute-start(bf16[128,1280]{1,0:T(8,128)(2,1)S(1)} %slice_bitcast_fusion.3), channel_id=1, source_target_pairs={{0,1},{1,0},{2,3},{3,2},{4,5},{5,4},{6,7},{7,6},{8,9},{9,8},{10,11... | collective-permute-start | bytes 983048 | tf_op jit(solution)/shard_map/ppermute | solution.py:42
  169.4 10.9 %all_to_all.5.grams = bf16[8,128,128]{2,1,0:T(8,128)(2,1)S(1)} all-to-all(bf16[8,128,128]{2,1,0:T(8,128)(2,1)S(1)} %get-tuple-element.90), channel_id=1, replica_groups=mesh['z'=8,'y'=4,'x'=4,'core'=2] {'x','core'}, dimensions={0} | all-to-all | bytes 524288 | tf_op jit(solution)/shard_map/all_to_all | solution.py:284
  180.3 3.5 %finish.1 = (bf16[128,3584]{1,0:T(8,128)(2,1)}, f32[1,128]{1,0:T(1,128)}) custom-call(bf16[8,128,128]{2,1,0:T(8,128)(2,1)S(1)} %all_to_all.5.grams, f32[1,128]{1,0:T(1,128)S(1)} %bitcast.62, bf16[128,3584]{1,0:T(8,128)(2,1)S(1)} %get-tuple-element.91.panel), custom_call_target="tpu_custom_call" | custom-call | tf_op jit(solution)/shard_map/finish/pallas_call | solution.py:220
  (96 shorter events, 60.7 us)
Async XLA Ops:
  1.8 13.8 %collective-permute-start.7 = (bf16[256,1024]{1,0:T(8,128)(2,1)S(1)}, bf16[256,1024]{1,0:T(8,128)(2,1)S(1)}, u32[]{:S(2)}, u32[]{:S(2)}) collective-permute-start(bf16[256,1024]{1,0:T(8,128)(2,1)S(1)} %get-tuple-element.100.part), channel_id=1, source_target_pairs={{0,1},{1,0},{2,3},{3,2},{4,5},{5,4},{6,7},{7,6},{8,9},{9,8},{10,11... | collective-permute-start | bytes 1572872 | tf_op jit(solution)/shard_map/ppermute | solution.py:42
  15.7 14.0 %collective-permute-start.8 = (bf16[2,256,1024]{2,1,0:T(8,128)(2,1)S(1)}, bf16[2,256,1024]{2,1,0:T(8,128)(2,1)S(1)}, u32[]{:S(2)}, u32[]{:S(2)}) collective-permute-start(bf16[2,256,1024]{2,1,0:T(8,128)(2,1)S(1)} %pad_maximum_fusion.5), channel_id=1, source_target_pairs={{0,8},{1,25},{8,16},{9,1},{16,24},{17,9},{24,0},{25,17},{2,10},{3,... | collective-permute-start | bytes 3145736 | tf_op jit(solution)/shard_map/ppermute | solution.py:48
  21.1 8.7 %collective-permute-start.4 = (bf16[2,3,32,1024]{3,2,1,0:T(8,128)(2,1)S(1)}, bf16[2,3,32,1024]{3,2,1,0:T(8,128)(2,1)S(1)}, u32[]{:S(2)}, u32[]{:S(2)}) collective-permute-start(bf16[2,3,32,1024]{3,2,1,0:T(8,128)(2,1)S(1)} %pad_maximum_fusion.10.both), channel_id=1, source_target_pairs={{0,2},{1,7},{2,4},{3,1},{4,6},{5,3},{6,0},{7,5},{8,10},{9,15},{10,... | collective-permute-start | bytes 1179656 | tf_op jit(solution)/shard_map/ppermute | solution.py:48
  21.9 11.2 %collective-permute-start.15 = (bf16[256,1280]{1,0:T(8,128)(2,1)S(1)}, bf16[256,1280]{1,0:T(8,128)(2,1)S(1)}, u32[]{:S(2)}, u32[]{:S(2)}) collective-permute-start(bf16[256,1280]{1,0:T(8,128)(2,1)S(1)} %get-tuple-element.65.part), channel_id=1, source_target_pairs={{0,1},{1,0},{2,3},{3,2},{4,5},{5,4},{6,7},{7,6},{8,9},{9,8},{10,11... | collective-permute-start | bytes 1966088 | tf_op jit(solution)/shard_map/ppermute | solution.py:42
  22.1 32.4 %collective-permute-start.20 = (bf16[2,256,1280]{2,1,0:T(8,128)(2,1)S(1)}, bf16[2,256,1280]{2,1,0:T(8,128)(2,1)S(1)}, u32[]{:S(2)}, u32[]{:S(2)}) collective-permute-start(bf16[2,256,1280]{2,1,0:T(8,128)(2,1)S(1)} %pad_maximum_fusion.4), channel_id=1, source_target_pairs={{0,8},{1,25},{8,16},{9,1},{16,24},{17,9},{24,0},{25,17},{2,10},{3,... | collective-permute-start | bytes 3932168 | tf_op jit(solution)/shard_map/ppermute | solution.py:48
  29.8 19.6 %collective-permute-start.9 = (bf16[256,1024]{1,0:T(8,128)(2,1)S(1)}, bf16[256,1024]{1,0:T(8,128)(2,1)S(1)}, u32[]{:S(2)}, u32[]{:S(2)}) collective-permute-start(bf16[256,1024]{1,0:T(8,128)(2,1)S(1)} %slice_bitcast_fusion.2), channel_id=1, source_target_pairs={{0,8},{1,25},{8,16},{9,1},{16,24},{17,9},{24,0},{25,17},{2,10},{3,... | collective-permute-start | bytes 1572872 | tf_op jit(solution)/shard_map/ppermute | solution.py:48
  33.3 30.2 %collective-permute-start.16 = (bf16[2,256,1280]{2,1,0:T(8,128)(2,1)S(1)}, bf16[2,256,1280]{2,1,0:T(8,128)(2,1)S(1)}, u32[]{:S(2)}, u32[]{:S(2)}) collective-permute-start(bf16[2,256,1280]{2,1,0:T(8,128)(2,1)S(1)} %pad_maximum_fusion.3), channel_id=1, source_target_pairs={{0,8},{1,25},{8,16},{9,1},{16,24},{17,9},{24,0},{25,17},{2,10},{3,... | collective-permute-start | bytes 3932168 | tf_op jit(solution)/shard_map/ppermute | solution.py:48
  37.5 15.9 %collective-permute-start.6 = (bf16[3,3,32,1024]{3,2,1,0:T(8,128)(2,1)S(1)}, bf16[3,3,32,1024]{3,2,1,0:T(8,128)(2,1)S(1)}, u32[]{:S(2)}, u32[]{:S(2)}) collective-permute-start(bf16[3,3,32,1024]{3,2,1,0:T(8,128)(2,1)S(1)} %pad_maximum_fusion.8), channel_id=1, source_target_pairs={{0,1},{1,0},{2,3},{3,2},{4,5},{5,4},{6,7},{7,6},{8,9},{9,8},{10,11... | collective-permute-start | bytes 1769480 | tf_op jit(solution)/shard_map/ppermute | solution.py:42
  49.5 13.9 %collective-permute-start.10 = (bf16[3,256,1024]{2,1,0:T(8,128)(2,1)S(1)}, bf16[3,256,1024]{2,1,0:T(8,128)(2,1)S(1)}, u32[]{:S(2)}, u32[]{:S(2)}) collective-permute-start(bf16[3,256,1024]{2,1,0:T(8,128)(2,1)S(1)} %pad_maximum_fusion.2), channel_id=1, source_target_pairs={{0,1},{1,0},{2,3},{3,2},{4,5},{5,4},{6,7},{7,6},{8,9},{9,8},{10,11... | collective-permute-start | bytes 4718600 | tf_op jit(solution)/shard_map/ppermute | solution.py:42
  54.5 15.9 %collective-permute-start.21 = (bf16[256,1280]{1,0:T(8,128)(2,1)S(1)}, bf16[256,1280]{1,0:T(8,128)(2,1)S(1)}, u32[]{:S(2)}, u32[]{:S(2)}) collective-permute-start(bf16[256,1280]{1,0:T(8,128)(2,1)S(1)} %slice_bitcast_fusion), channel_id=1, source_target_pairs={{0,8},{1,25},{8,16},{9,1},{16,24},{17,9},{24,0},{25,17},{2,10},{3,... | collective-permute-start | bytes 1966088 | tf_op jit(solution)/shard_map/ppermute | solution.py:48
  66.4 12.0 %collective-permute-start.17 = (bf16[256,1280]{1,0:T(8,128)(2,1)S(1)}, bf16[256,1280]{1,0:T(8,128)(2,1)S(1)}, u32[]{:S(2)}, u32[]{:S(2)}) collective-permute-start(bf16[256,1280]{1,0:T(8,128)(2,1)S(1)} %slice_bitcast_fusion.1), channel_id=1, source_target_pairs={{0,8},{1,25},{8,16},{9,1},{16,24},{17,9},{24,0},{25,17},{2,10},{3,... | collective-permute-start | bytes 1966088 | tf_op jit(solution)/shard_map/ppermute | solution.py:48
  70.6 25.3 %collective-permute-start.22 = (bf16[3,256,1280]{2,1,0:T(8,128)(2,1)S(1)}, bf16[3,256,1280]{2,1,0:T(8,128)(2,1)S(1)}, u32[]{:S(2)}, u32[]{:S(2)}) collective-permute-start(bf16[3,256,1280]{2,1,0:T(8,128)(2,1)S(1)} %pad_maximum_fusion), channel_id=1, source_target_pairs={{0,1},{1,0},{2,3},{3,2},{4,5},{5,4},{6,7},{7,6},{8,9},{9,8},{10,11... | collective-permute-start | bytes 5898248 | tf_op jit(solution)/shard_map/ppermute | solution.py:42
  78.5 27.0 %collective-permute-start.28 = (bf16[3,256,1280]{2,1,0:T(8,128)(2,1)S(1)}, bf16[3,256,1280]{2,1,0:T(8,128)(2,1)S(1)}, u32[]{:S(2)}, u32[]{:S(2)}) collective-permute-start(bf16[3,256,1280]{2,1,0:T(8,128)(2,1)S(1)} %pad_maximum_fusion.1), channel_id=1, source_target_pairs={{0,1},{1,0},{2,3},{3,2},{4,5},{5,4},{6,7},{7,6},{8,9},{9,8},{10,11... | collective-permute-start | bytes 5898248 | tf_op jit(solution)/shard_map/ppermute | solution.py:42
  82.5 10.0 %collective-permute-start.12 = (bf16[2,128,1024]{2,1,0:T(8,128)(2,1)S(1)}, bf16[2,128,1024]{2,1,0:T(8,128)(2,1)S(1)}, u32[]{:S(2)}, u32[]{:S(2)}) collective-permute-start(bf16[2,128,1024]{2,1,0:T(8,128)(2,1)S(1)} %pad_maximum_fusion.9), channel_id=1, source_target_pairs={{0,32},{1,225},{32,64},{33,1},{64,96},{65,33},{96,128},{97,65},{12... | collective-permute-start | bytes 1572872 | tf_op jit(solution)/shard_map/ppermute | solution.py:48
  92.8 9.3 %collective-permute-start.13 = (bf16[2,128,1024]{2,1,0:T(8,128)(2,1)S(1)}, bf16[2,128,1024]{2,1,0:T(8,128)(2,1)S(1)}, u32[]{:S(2)}, u32[]{:S(2)}) collective-permute-start(bf16[2,128,1024]{2,1,0:T(8,128)(2,1)S(1)} %add_convert_fusion.5), channel_id=1, source_target_pairs={{0,32},{1,225},{32,64},{33,1},{64,96},{65,33},{96,128},{97,65},{12... | collective-permute-start | bytes 1572872 | tf_op jit(solution)/shard_map/ppermute | solution.py:48
  99.6 9.7 %collective-permute-start.23 = (bf16[128,1280]{1,0:T(8,128)(2,1)S(1)}, bf16[128,1280]{1,0:T(8,128)(2,1)S(1)}, u32[]{:S(2)}, u32[]{:S(2)}) collective-permute-start(bf16[128,1280]{1,0:T(8,128)(2,1)S(1)} %get-tuple-element.74), channel_id=1, source_target_pairs={{0,32},{1,225},{32,64},{33,1},{64,96},{65,33},{96,128},{97,65},{12... | collective-permute-start | bytes 983048 | tf_op jit(solution)/shard_map/ppermute | solution.py:48
  102.3 13.3 %collective-permute-start.18 = (bf16[2,128,1024]{2,1,0:T(8,128)(2,1)S(1)}, bf16[2,128,1024]{2,1,0:T(8,128)(2,1)S(1)}, u32[]{:S(2)}, u32[]{:S(2)}) collective-permute-start(bf16[2,128,1024]{2,1,0:T(8,128)(2,1)S(1)} %add_convert_fusion.4), channel_id=1, source_target_pairs={{0,32},{1,225},{32,64},{33,1},{64,96},{65,33},{96,128},{97,65},{12... | collective-permute-start | bytes 1572872 | tf_op jit(solution)/shard_map/ppermute | solution.py:48
  109.4 13.1 %collective-permute-start.24 = (bf16[2,128,1280]{2,1,0:T(8,128)(2,1)S(1)}, bf16[2,128,1280]{2,1,0:T(8,128)(2,1)S(1)}, u32[]{:S(2)}, u32[]{:S(2)}) collective-permute-start(bf16[2,128,1280]{2,1,0:T(8,128)(2,1)S(1)} %pad_maximum_fusion.6), channel_id=1, source_target_pairs={{0,32},{1,225},{32,64},{33,1},{64,96},{65,33},{96,128},{97,65},{12... | collective-permute-start | bytes 1966088 | tf_op jit(solution)/shard_map/ppermute | solution.py:48
  115.6 13.9 %collective-permute-start.30 = (bf16[2,128,1280]{2,1,0:T(8,128)(2,1)S(1)}, bf16[2,128,1280]{2,1,0:T(8,128)(2,1)S(1)}, u32[]{:S(2)}, u32[]{:S(2)}) collective-permute-start(bf16[2,128,1280]{2,1,0:T(8,128)(2,1)S(1)} %pad_maximum_fusion.7), channel_id=1, source_target_pairs={{0,32},{1,225},{32,64},{33,1},{64,96},{65,33},{96,128},{97,65},{12... | collective-permute-start | bytes 1966088 | tf_op jit(solution)/shard_map/ppermute | solution.py:48
  122.6 13.9 %collective-permute-start.25 = (bf16[2,128,1280]{2,1,0:T(8,128)(2,1)S(1)}, bf16[2,128,1280]{2,1,0:T(8,128)(2,1)S(1)}, u32[]{:S(2)}, u32[]{:S(2)}) collective-permute-start(bf16[2,128,1280]{2,1,0:T(8,128)(2,1)S(1)} %add_convert_fusion.3), channel_id=1, source_target_pairs={{0,32},{1,225},{32,64},{33,1},{64,96},{65,33},{96,128},{97,65},{12... | collective-permute-start | bytes 1966088 | tf_op jit(solution)/shard_map/ppermute | solution.py:48
  136.5 10.3 %collective-permute-start.31 = (bf16[2,128,1280]{2,1,0:T(8,128)(2,1)S(1)}, bf16[2,128,1280]{2,1,0:T(8,128)(2,1)S(1)}, u32[]{:S(2)}, u32[]{:S(2)}) collective-permute-start(bf16[2,128,1280]{2,1,0:T(8,128)(2,1)S(1)} %add_convert_fusion.1), channel_id=1, source_target_pairs={{0,32},{1,225},{32,64},{33,1},{64,96},{65,33},{96,128},{97,65},{12... | collective-permute-start | bytes 1966088 | tf_op jit(solution)/shard_map/ppermute | solution.py:48
  139.4 14.4 %collective-permute-start.26 = (bf16[2,128,1280]{2,1,0:T(8,128)(2,1)S(1)}, bf16[2,128,1280]{2,1,0:T(8,128)(2,1)S(1)}, u32[]{:S(2)}, u32[]{:S(2)}) collective-permute-start(bf16[2,128,1280]{2,1,0:T(8,128)(2,1)S(1)} %add_convert_fusion.2), channel_id=1, source_target_pairs={{0,32},{1,225},{32,64},{33,1},{64,96},{65,33},{96,128},{97,65},{12... | collective-permute-start | bytes 1966088 | tf_op jit(solution)/shard_map/ppermute | solution.py:48
  147.0 13.9 %collective-permute-start.32 = (bf16[2,128,1280]{2,1,0:T(8,128)(2,1)S(1)}, bf16[2,128,1280]{2,1,0:T(8,128)(2,1)S(1)}, u32[]{:S(2)}, u32[]{:S(2)}) collective-permute-start(bf16[2,128,1280]{2,1,0:T(8,128)(2,1)S(1)} %add_convert_fusion), channel_id=1, source_target_pairs={{0,32},{1,225},{32,64},{33,1},{64,96},{65,33},{96,128},{97,65},{12... | collective-permute-start | bytes 1966088 | tf_op jit(solution)/shard_map/ppermute | solution.py:48
  153.9 13.5 %collective-permute-start.27 = (bf16[128,1280]{1,0:T(8,128)(2,1)S(1)}, bf16[128,1280]{1,0:T(8,128)(2,1)S(1)}, u32[]{:S(2)}, u32[]{:S(2)}) collective-permute-start(bf16[128,1280]{1,0:T(8,128)(2,1)S(1)} %slice_bitcast_fusion.4), channel_id=1, source_target_pairs={{0,1},{1,0},{2,3},{3,2},{4,5},{5,4},{6,7},{7,6},{8,9},{9,8},{10,11... | collective-permute-start | bytes 983048 | tf_op jit(solution)/shard_map/ppermute | solution.py:42
  (15 other events, 92.5 us)

commit v2 on v1

--- a/solution.py
+++ b/solution.py
@@ -233,9 +233,11 @@
     place = jnp.stack([z, y, core, x, x * NC + core]).astype(jnp.int32)
     n = len(CHUNKS)
     starts = [sum(CHUNKS[:i]) for i in range(n)]
+    sources = source(place, out_grad)
+    hidden = after(hidden, sources[0])
     part = [hidden[:, i:i + width] for i, width in zip(starts, CHUNKS)]
     sibling, near, far, other, made, ring = [[None] * n for _ in range(6)]
-    got = jnp.stack([shifted(a, "y", by) for a, by in zip(source(place, out_grad), (1, -1, 2))])
+    got = jnp.stack([shifted(a, "y", by) for a, by in zip(sources, (1, -1, 2))])
     both = jnp.stack([got, core_swapped(got)])
     for i in range(n):
         sibling[i] = core_swapped(after(part[i], sibling[i - 1]) if i else part[i])

time: 184 us -> 184 us (level)
  starting transfers between devices: 69.5 us -> 71.4 us
    ppermute x11, starting transfers between devices: 29.5 us -> 33 us  [core_swapped(): return lax.ppermute(x, 'core', [(0, 1), (1, 0)])]
  transfers between devices with their start and end apart: 34 -> 34, of which waited for: 19 -> 19; matrix products, arithmetic and copies ran while one was open for 2% -> 1% of each run, Pallas kernels for 7% -> 6%
where the time goes in v2:
time: 184 us; the launch traced here: 183 us
  waiting for transfers between devices  77.4 us (42%)
  starting transfers between devices  71.4 us (39%)
  Pallas kernels  19 us (10%)
  blocking collectives  10.9 us (6%)
  other arithmetic  2.33 us (1%)
    ppermute x20, waiting for transfers between devices, around(): return lax.ppermute(x, (axis, 'core'), pairs)  69.3 us
    ppermute x20, starting transfers between devices, around(): return lax.ppermute(x, (axis, 'core'), pairs)  35.8 us
    ppermute x11, starting transfers between devices, core_swapped(): return lax.ppermute(x, 'core', [(0, 1), (1, 0)])  33 us
    all_to_all x1, blocking collectives, body(): grams = lax.all_to_all(grams, TENSOR, 0, 0, tiled=True)  10.9 us
    pallas_call x3, Pallas kernels, product(): pl.pallas_call(product_kernel, in_specs=[VMEM] * 6, out_specs=[VMEM] * 5,...  10.1 us
    ppermute x3, waiting for transfers between devices, shifted(): return lax.ppermute(x, axis, [(i, (i + by) % count) for i in range(count)])  4.62 us
  transfers between devices with their start and end apart: 34, of which 19 were waited for; matrix products, arithmetic and copies ran while one was open for 1% of the time, Pallas kernels for 6%

profile of v2, /device:TPU:1, one launch (start us, length us, event | category | flops | bytes accessed | tf_op | source)
XLA Modules:
  0.0 183.3 jit_solution(8498254891645605362)
XLA Ops:
  3.8 3.3 %collective-permute-start.7 = (bf16[256,1024]{1,0:T(8,128)(2,1)S(1)}, bf16[256,1024]{1,0:T(8,128)(2,1)S(1)}, u32[]{:S(2)}, u32[]{:S(2)}) collective-permute-start(bf16[256,1024]{1,0:T(8,128)(2,1)S(1)} %get-tuple-element.102.part), channel_id=1, source_target_pairs={{0,1},{1,0},{2,3},{3,2},{4,5},{5,4},{6,7},{7,6},{8,9},{9,8},{10,11... | collective-permute-start | bytes 1572872 | tf_op jit(solution)/shard_map/ppermute | solution.py:42
  23.3 5.3 %collective-permute-done.8.near = bf16[2,256,1024]{2,1,0:T(8,128)(2,1)S(1)} collective-permute-done((bf16[2,256,1024]{2,1,0:T(8,128)(2,1)S(1)}, bf16[2,256,1024]{2,1,0:T(8,128)(2,1)S(1)}, u32[]{:S(2)}, u32[]{:S(2)}) %collective-permute-start.8) | collective-permute-done | bytes 1048608 | tf_op jit(solution)/shard_map/ppermute | solution.py:48
  35.3 4.9 %collective-permute-start.6 = (bf16[3,3,32,1024]{3,2,1,0:T(8,128)(2,1)S(1)}, bf16[3,3,32,1024]{3,2,1,0:T(8,128)(2,1)S(1)}, u32[]{:S(2)}, u32[]{:S(2)}) collective-permute-start(bf16[3,3,32,1024]{3,2,1,0:T(8,128)(2,1)S(1)} %pad_maximum_fusion.8), channel_id=1, source_target_pairs={{0,1},{1,0},{2,3},{3,2},{4,5},{5,4},{6,7},{7,6},{8,9},{9,8},{10,11... | collective-permute-start | bytes 1769480 | tf_op jit(solution)/shard_map/ppermute | solution.py:42
  40.2 8.0 %collective-permute-done.9.far = bf16[256,1024]{1,0:T(8,128)(2,1)S(1)} collective-permute-done((bf16[256,1024]{1,0:T(8,128)(2,1)S(1)}, bf16[256,1024]{1,0:T(8,128)(2,1)S(1)}, u32[]{:S(2)}, u32[]{:S(2)}) %collective-permute-start.9) | collective-permute-done | bytes 524320 | tf_op jit(solution)/shard_map/ppermute | solution.py:48
  48.4 4.5 %collective-permute-start.10 = (bf16[3,256,1024]{2,1,0:T(8,128)(2,1)S(1)}, bf16[3,256,1024]{2,1,0:T(8,128)(2,1)S(1)}, u32[]{:S(2)}, u32[]{:S(2)}) collective-permute-start(bf16[3,256,1024]{2,1,0:T(8,128)(2,1)S(1)} %pad_maximum_fusion.2), channel_id=1, source_target_pairs={{0,1},{1,0},{2,3},{3,2},{4,5},{5,4},{6,7},{7,6},{8,9},{9,8},{10,11... | collective-permute-start | bytes 4718600 | tf_op jit(solution)/shard_map/ppermute | solution.py:42
  54.3 8.0 %collective-permute-done.16.near = bf16[2,256,1280]{2,1,0:T(8,128)(2,1)S(1)} collective-permute-done((bf16[2,256,1280]{2,1,0:T(8,128)(2,1)S(1)}, bf16[2,256,1280]{2,1,0:T(8,128)(2,1)S(1)}, u32[]{:S(2)}, u32[]{:S(2)}) %collective-permute-start.16) | collective-permute-done | bytes 1310752 | tf_op jit(solution)/shard_map/ppermute | solution.py:48
  69.5 4.5 %collective-permute-start.22 = (bf16[3,256,1280]{2,1,0:T(8,128)(2,1)S(1)}, bf16[3,256,1280]{2,1,0:T(8,128)(2,1)S(1)}, u32[]{:S(2)}, u32[]{:S(2)}) collective-permute-start(bf16[3,256,1280]{2,1,0:T(8,128)(2,1)S(1)} %pad_maximum_fusion), channel_id=1, source_target_pairs={{0,1},{1,0},{2,3},{3,2},{4,5},{5,4},{6,7},{7,6},{8,9},{9,8},{10,11... | collective-permute-start | bytes 5898248 | tf_op jit(solution)/shard_map/ppermute | solution.py:42
  74.0 3.8 %collective-permute-start.11 = (bf16[128,1024]{1,0:T(8,128)(2,1)S(1)}, bf16[128,1024]{1,0:T(8,128)(2,1)S(1)}, u32[]{:S(2)}, u32[]{:S(2)}) collective-permute-start(bf16[128,1024]{1,0:T(8,128)(2,1)S(1)} %get-tuple-element.60), channel_id=1, source_target_pairs={{0,32},{1,225},{32,64},{33,1},{64,96},{65,33},{96,128},{97,65},{12... | collective-permute-start | bytes 786440 | tf_op jit(solution)/shard_map/ppermute | solution.py:48
  78.0 3.8 %collective-permute-start.28 = (bf16[3,256,1280]{2,1,0:T(8,128)(2,1)S(1)}, bf16[3,256,1280]{2,1,0:T(8,128)(2,1)S(1)}, u32[]{:S(2)}, u32[]{:S(2)}) collective-permute-start(bf16[3,256,1280]{2,1,0:T(8,128)(2,1)S(1)} %pad_maximum_fusion.1), channel_id=1, source_target_pairs={{0,1},{1,0},{2,3},{3,2},{4,5},{5,4},{6,7},{7,6},{8,9},{9,8},{10,11... | collective-permute-start | bytes 5898248 | tf_op jit(solution)/shard_map/ppermute | solution.py:42
  81.9 3.9 %collective-permute-start.12 = (bf16[2,128,1024]{2,1,0:T(8,128)(2,1)S(1)}, bf16[2,128,1024]{2,1,0:T(8,128)(2,1)S(1)}, u32[]{:S(2)}, u32[]{:S(2)}) collective-permute-start(bf16[2,128,1024]{2,1,0:T(8,128)(2,1)S(1)} %pad_maximum_fusion.9), channel_id=1, source_target_pairs={{0,32},{1,225},{32,64},{33,1},{64,96},{65,33},{96,128},{97,65},{12... | collective-permute-start | bytes 1572872 | tf_op jit(solution)/shard_map/ppermute | solution.py:48
  85.9 6.1 %collective-permute-done.12 = bf16[2,128,1024]{2,1,0:T(8,128)(2,1)S(1)} collective-permute-done((bf16[2,128,1024]{2,1,0:T(8,128)(2,1)S(1)}, bf16[2,128,1024]{2,1,0:T(8,128)(2,1)S(1)}, u32[]{:S(2)}, u32[]{:S(2)}) %collective-permute-start.12) | collective-permute-done | bytes 524320 | tf_op jit(solution)/shard_map/ppermute | solution.py:48
  95.4 3.6 %product.4 = (bf16[2,128,1280]{2,1,0:T(8,128)(2,1)S(1)}, bf16[2,128,1280]{2,1,0:T(8,128)(2,1)S(1)}, bf16[2,128,1280]{2,1,0:T(8,128)(2,1)S(1)}, bf16[128,1280]{1,0:T(8,128)(2,1)S(1)}, bf16[128,1280]{1,0:T(8,128)(2,1)S(1)}) custom-call(bf16[640,1024]{1,0:T(8,128)(2,1)S(1)} %turn.1.turned, bf16[256,1280]{1,0:T(8,128)(2,1)S(1)} %get-tuple-element.66.part, ...), custom_call_target="tpu_custom_call" | custom-call | flops 2684354560 | bytes 3932160 | tf_op jit(solution)/shard_map/product/pallas_call | solution.py:143
  104.9 3.6 %product.5 = (bf16[2,128,1280]{2,1,0:T(8,128)(2,1)S(1)}, bf16[2,128,1280]{2,1,0:T(8,128)(2,1)S(1)}, bf16[2,128,1280]{2,1,0:T(8,128)(2,1)S(1)}, bf16[128,1280]{1,0:T(8,128)(2,1)S(1)}, bf16[128,1280]{1,0:T(8,128)(2,1)S(1)}) custom-call(bf16[640,1024]{1,0:T(8,128)(2,1)S(1)} %turn.1.turned, bf16[256,1280]{1,0:T(8,128)(2,1)S(1)} %get-tuple-element.67.part, ...), custom_call_target="tpu_custom_call" | custom-call | flops 2684354560 | bytes 3932160 | tf_op jit(solution)/shard_map/product/pallas_call | solution.py:143
  108.9 5.9 %collective-permute-done.29 = bf16[128,1280]{1,0:T(8,128)(2,1)S(1)} collective-permute-done((bf16[128,1280]{1,0:T(8,128)(2,1)S(1)}, bf16[128,1280]{1,0:T(8,128)(2,1)S(1)}, u32[]{:S(2)}, u32[]{:S(2)}) %collective-permute-start.29) | collective-permute-done | bytes 327712 | tf_op jit(solution)/shard_map/ppermute | solution.py:48
  117.9 4.0 %collective-permute-done.24 = bf16[2,128,1280]{2,1,0:T(8,128)(2,1)S(1)} collective-permute-done((bf16[2,128,1280]{2,1,0:T(8,128)(2,1)S(1)}, bf16[2,128,1280]{2,1,0:T(8,128)(2,1)S(1)}, u32[]{:S(2)}, u32[]{:S(2)}) %collective-permute-start.24) | collective-permute-done | bytes 655392 | tf_op jit(solution)/shard_map/ppermute | solution.py:48
  124.9 4.0 %collective-permute-done.30 = bf16[2,128,1280]{2,1,0:T(8,128)(2,1)S(1)} collective-permute-done((bf16[2,128,1280]{2,1,0:T(8,128)(2,1)S(1)}, bf16[2,128,1280]{2,1,0:T(8,128)(2,1)S(1)}, u32[]{:S(2)}, u32[]{:S(2)}) %collective-permute-start.30) | collective-permute-done | bytes 655392 | tf_op jit(solution)/shard_map/ppermute | solution.py:48
  129.1 6.9 %collective-permute-done.25 = bf16[2,128,1280]{2,1,0:T(8,128)(2,1)S(1)} collective-permute-done((bf16[2,128,1280]{2,1,0:T(8,128)(2,1)S(1)}, bf16[2,128,1280]{2,1,0:T(8,128)(2,1)S(1)}, u32[]{:S(2)}, u32[]{:S(2)}) %collective-permute-start.25) | collective-permute-done | bytes 655392 | tf_op jit(solution)/shard_map/ppermute | solution.py:48
  139.0 7.3 %collective-permute-done.31 = bf16[2,128,1280]{2,1,0:T(8,128)(2,1)S(1)} collective-permute-done((bf16[2,128,1280]{2,1,0:T(8,128)(2,1)S(1)}, bf16[2,128,1280]{2,1,0:T(8,128)(2,1)S(1)}, u32[]{:S(2)}, u32[]{:S(2)}) %collective-permute-start.31) | collective-permute-done | bytes 655392 | tf_op jit(solution)/shard_map/ppermute | solution.py:48
  146.4 3.2 %collective-permute-start.32 = (bf16[2,128,1280]{2,1,0:T(8,128)(2,1)S(1)}, bf16[2,128,1280]{2,1,0:T(8,128)(2,1)S(1)}, u32[]{:S(2)}, u32[]{:S(2)}) collective-permute-start(bf16[2,128,1280]{2,1,0:T(8,128)(2,1)S(1)} %add_convert_fusion), channel_id=1, source_target_pairs={{0,32},{1,225},{32,64},{33,1},{64,96},{65,33},{96,128},{97,65},{12... | collective-permute-start | bytes 1966088 | tf_op jit(solution)/shard_map/ppermute | solution.py:48
  149.6 3.7 %collective-permute-done.26.refs_4_ = bf16[2,128,1280]{2,1,0:T(8,128)(2,1)S(1)} collective-permute-done((bf16[2,128,1280]{2,1,0:T(8,128)(2,1)S(1)}, bf16[2,128,1280]{2,1,0:T(8,128)(2,1)S(1)}, u32[]{:S(2)}, u32[]{:S(2)}) %collective-permute-start.26) | collective-permute-done | bytes 655392 | tf_op jit(solution)/shard_map/ppermute | solution.py:48
  153.3 4.9 %collective-permute-start.27 = (bf16[128,1280]{1,0:T(8,128)(2,1)S(1)}, bf16[128,1280]{1,0:T(8,128)(2,1)S(1)}, u32[]{:S(2)}, u32[]{:S(2)}) collective-permute-start(bf16[128,1280]{1,0:T(8,128)(2,1)S(1)} %slice_bitcast_fusion.4), channel_id=1, source_target_pairs={{0,1},{1,0},{2,3},{3,2},{4,5},{5,4},{6,7},{7,6},{8,9},{9,8},{10,11... | collective-permute-start | bytes 983048 | tf_op jit(solution)/shard_map/ppermute | solution.py:42
  160.3 4.9 %collective-permute-start.33 = (bf16[128,1280]{1,0:T(8,128)(2,1)S(1)}, bf16[128,1280]{1,0:T(8,128)(2,1)S(1)}, u32[]{:S(2)}, u32[]{:S(2)}) collective-permute-start(bf16[128,1280]{1,0:T(8,128)(2,1)S(1)} %slice_bitcast_fusion.3), channel_id=1, source_target_pairs={{0,1},{1,0},{2,3},{3,2},{4,5},{5,4},{6,7},{7,6},{8,9},{9,8},{10,11... | collective-permute-start | bytes 983048 | tf_op jit(solution)/shard_map/ppermute | solution.py:42
  168.8 10.9 %all_to_all.5.grams = bf16[8,128,128]{2,1,0:T(8,128)(2,1)S(1)} all-to-all(bf16[8,128,128]{2,1,0:T(8,128)(2,1)S(1)} %get-tuple-element.92), channel_id=1, replica_groups=mesh['z'=8,'y'=4,'x'=4,'core'=2] {'x','core'}, dimensions={0} | all-to-all | bytes 524288 | tf_op jit(solution)/shard_map/all_to_all | solution.py:286
  179.8 3.5 %finish.1 = (bf16[128,3584]{1,0:T(8,128)(2,1)}, f32[1,128]{1,0:T(1,128)}) custom-call(bf16[8,128,128]{2,1,0:T(8,128)(2,1)S(1)} %all_to_all.5.grams, f32[1,128]{1,0:T(1,128)S(1)} %bitcast.62, bf16[128,3584]{1,0:T(8,128)(2,1)S(1)} %get-tuple-element.93.panel), custom_call_target="tpu_custom_call" | custom-call | tf_op jit(solution)/shard_map/finish/pallas_call | solution.py:220
  (102 shorter events, 59.7 us)
Async XLA Ops:
  3.8 10.7 %collective-permute-start.7 = (bf16[256,1024]{1,0:T(8,128)(2,1)S(1)}, bf16[256,1024]{1,0:T(8,128)(2,1)S(1)}, u32[]{:S(2)}, u32[]{:S(2)}) collective-permute-start(bf16[256,1024]{1,0:T(8,128)(2,1)S(1)} %get-tuple-element.102.part), channel_id=1, source_target_pairs={{0,1},{1,0},{2,3},{3,2},{4,5},{5,4},{6,7},{7,6},{8,9},{9,8},{10,11... | collective-permute-start | bytes 1572872 | tf_op jit(solution)/shard_map/ppermute | solution.py:42
  14.6 14.0 %collective-permute-start.8 = (bf16[2,256,1024]{2,1,0:T(8,128)(2,1)S(1)}, bf16[2,256,1024]{2,1,0:T(8,128)(2,1)S(1)}, u32[]{:S(2)}, u32[]{:S(2)}) collective-permute-start(bf16[2,256,1024]{2,1,0:T(8,128)(2,1)S(1)} %pad_maximum_fusion.5), channel_id=1, source_target_pairs={{0,8},{1,25},{8,16},{9,1},{16,24},{17,9},{24,0},{25,17},{2,10},{3,... | collective-permute-start | bytes 3145736 | tf_op jit(solution)/shard_map/ppermute | solution.py:48
  19.3 9.3 %collective-permute-start.4 = (bf16[2,3,32,1024]{3,2,1,0:T(8,128)(2,1)S(1)}, bf16[2,3,32,1024]{3,2,1,0:T(8,128)(2,1)S(1)}, u32[]{:S(2)}, u32[]{:S(2)}) collective-permute-start(bf16[2,3,32,1024]{3,2,1,0:T(8,128)(2,1)S(1)} %pad_maximum_fusion.10.both), channel_id=1, source_target_pairs={{0,2},{1,7},{2,4},{3,1},{4,6},{5,3},{6,0},{7,5},{8,10},{9,15},{10,... | collective-permute-start | bytes 1179656 | tf_op jit(solution)/shard_map/ppermute | solution.py:48
  20.5 11.6 %collective-permute-start.15 = (bf16[256,1280]{1,0:T(8,128)(2,1)S(1)}, bf16[256,1280]{1,0:T(8,128)(2,1)S(1)}, u32[]{:S(2)}, u32[]{:S(2)}) collective-permute-start(bf16[256,1280]{1,0:T(8,128)(2,1)S(1)} %get-tuple-element.67.part), channel_id=1, source_target_pairs={{0,1},{1,0},{2,3},{3,2},{4,5},{5,4},{6,7},{7,6},{8,9},{9,8},{10,11... | collective-permute-start | bytes 1966088 | tf_op jit(solution)/shard_map/ppermute | solution.py:42
  20.6 33.3 %collective-permute-start.20 = (bf16[2,256,1280]{2,1,0:T(8,128)(2,1)S(1)}, bf16[2,256,1280]{2,1,0:T(8,128)(2,1)S(1)}, u32[]{:S(2)}, u32[]{:S(2)}) collective-permute-start(bf16[2,256,1280]{2,1,0:T(8,128)(2,1)S(1)} %pad_maximum_fusion.4), channel_id=1, source_target_pairs={{0,8},{1,25},{8,16},{9,1},{16,24},{17,9},{24,0},{25,17},{2,10},{3,... | collective-permute-start | bytes 3932168 | tf_op jit(solution)/shard_map/ppermute | solution.py:48
  28.6 19.6 %collective-permute-start.9 = (bf16[256,1024]{1,0:T(8,128)(2,1)S(1)}, bf16[256,1024]{1,0:T(8,128)(2,1)S(1)}, u32[]{:S(2)}, u32[]{:S(2)}) collective-permute-start(bf16[256,1024]{1,0:T(8,128)(2,1)S(1)} %slice_bitcast_fusion.2), channel_id=1, source_target_pairs={{0,8},{1,25},{8,16},{9,1},{16,24},{17,9},{24,0},{25,17},{2,10},{3,... | collective-permute-start | bytes 1572872 | tf_op jit(solution)/shard_map/ppermute | solution.py:48
  32.2 30.1 %collective-permute-start.16 = (bf16[2,256,1280]{2,1,0:T(8,128)(2,1)S(1)}, bf16[2,256,1280]{2,1,0:T(8,128)(2,1)S(1)}, u32[]{:S(2)}, u32[]{:S(2)}) collective-permute-start(bf16[2,256,1280]{2,1,0:T(8,128)(2,1)S(1)} %pad_maximum_fusion.3), channel_id=1, source_target_pairs={{0,8},{1,25},{8,16},{9,1},{16,24},{17,9},{24,0},{25,17},{2,10},{3,... | collective-permute-start | bytes 3932168 | tf_op jit(solution)/shard_map/ppermute | solution.py:48
  35.3 17.6 %collective-permute-start.6 = (bf16[3,3,32,1024]{3,2,1,0:T(8,128)(2,1)S(1)}, bf16[3,3,32,1024]{3,2,1,0:T(8,128)(2,1)S(1)}, u32[]{:S(2)}, u32[]{:S(2)}) collective-permute-start(bf16[3,3,32,1024]{3,2,1,0:T(8,128)(2,1)S(1)} %pad_maximum_fusion.8), channel_id=1, source_target_pairs={{0,1},{1,0},{2,3},{3,2},{4,5},{5,4},{6,7},{7,6},{8,9},{9,8},{10,11... | collective-permute-start | bytes 1769480 | tf_op jit(solution)/shard_map/ppermute | solution.py:42
  48.4 13.9 %collective-permute-start.10 = (bf16[3,256,1024]{2,1,0:T(8,128)(2,1)S(1)}, bf16[3,256,1024]{2,1,0:T(8,128)(2,1)S(1)}, u32[]{:S(2)}, u32[]{:S(2)}) collective-permute-start(bf16[3,256,1024]{2,1,0:T(8,128)(2,1)S(1)} %pad_maximum_fusion.2), channel_id=1, source_target_pairs={{0,1},{1,0},{2,3},{3,2},{4,5},{5,4},{6,7},{7,6},{8,9},{9,8},{10,11... | collective-permute-start | bytes 4718600 | tf_op jit(solution)/shard_map/ppermute | solution.py:42
  54.0 15.3 %collective-permute-start.21 = (bf16[256,1280]{1,0:T(8,128)(2,1)S(1)}, bf16[256,1280]{1,0:T(8,128)(2,1)S(1)}, u32[]{:S(2)}, u32[]{:S(2)}) collective-permute-start(bf16[256,1280]{1,0:T(8,128)(2,1)S(1)} %slice_bitcast_fusion), channel_id=1, source_target_pairs={{0,8},{1,25},{8,16},{9,1},{16,24},{17,9},{24,0},{25,17},{2,10},{3,... | collective-permute-start | bytes 1966088 | tf_op jit(solution)/shard_map/ppermute | solution.py:48
  65.3 12.5 %collective-permute-start.17 = (bf16[256,1280]{1,0:T(8,128)(2,1)S(1)}, bf16[256,1280]{1,0:T(8,128)(2,1)S(1)}, u32[]{:S(2)}, u32[]{:S(2)}) collective-permute-start(bf16[256,1280]{1,0:T(8,128)(2,1)S(1)} %slice_bitcast_fusion.1), channel_id=1, source_target_pairs={{0,8},{1,25},{8,16},{9,1},{16,24},{17,9},{24,0},{25,17},{2,10},{3,... | collective-permute-start | bytes 1966088 | tf_op jit(solution)/shard_map/ppermute | solution.py:48
  69.5 25.9 %collective-permute-start.22 = (bf16[3,256,1280]{2,1,0:T(8,128)(2,1)S(1)}, bf16[3,256,1280]{2,1,0:T(8,128)(2,1)S(1)}, u32[]{:S(2)}, u32[]{:S(2)}) collective-permute-start(bf16[3,256,1280]{2,1,0:T(8,128)(2,1)S(1)} %pad_maximum_fusion), channel_id=1, source_target_pairs={{0,1},{1,0},{2,3},{3,2},{4,5},{5,4},{6,7},{7,6},{8,9},{9,8},{10,11... | collective-permute-start | bytes 5898248 | tf_op jit(solution)/shard_map/ppermute | solution.py:42
  78.0 26.9 %collective-permute-start.28 = (bf16[3,256,1280]{2,1,0:T(8,128)(2,1)S(1)}, bf16[3,256,1280]{2,1,0:T(8,128)(2,1)S(1)}, u32[]{:S(2)}, u32[]{:S(2)}) collective-permute-start(bf16[3,256,1280]{2,1,0:T(8,128)(2,1)S(1)} %pad_maximum_fusion.1), channel_id=1, source_target_pairs={{0,1},{1,0},{2,3},{3,2},{4,5},{5,4},{6,7},{7,6},{8,9},{9,8},{10,11... | collective-permute-start | bytes 5898248 | tf_op jit(solution)/shard_map/ppermute | solution.py:42
  81.9 10.0 %collective-permute-start.12 = (bf16[2,128,1024]{2,1,0:T(8,128)(2,1)S(1)}, bf16[2,128,1024]{2,1,0:T(8,128)(2,1)S(1)}, u32[]{:S(2)}, u32[]{:S(2)}) collective-permute-start(bf16[2,128,1024]{2,1,0:T(8,128)(2,1)S(1)} %pad_maximum_fusion.9), channel_id=1, source_target_pairs={{0,32},{1,225},{32,64},{33,1},{64,96},{65,33},{96,128},{97,65},{12... | collective-permute-start | bytes 1572872 | tf_op jit(solution)/shard_map/ppermute | solution.py:48
  92.2 9.3 %collective-permute-start.13 = (bf16[2,128,1024]{2,1,0:T(8,128)(2,1)S(1)}, bf16[2,128,1024]{2,1,0:T(8,128)(2,1)S(1)}, u32[]{:S(2)}, u32[]{:S(2)}) collective-permute-start(bf16[2,128,1024]{2,1,0:T(8,128)(2,1)S(1)} %add_convert_fusion.5), channel_id=1, source_target_pairs={{0,32},{1,225},{32,64},{33,1},{64,96},{65,33},{96,128},{97,65},{12... | collective-permute-start | bytes 1572872 | tf_op jit(solution)/shard_map/ppermute | solution.py:48
  99.0 9.7 %collective-permute-start.23 = (bf16[128,1280]{1,0:T(8,128)(2,1)S(1)}, bf16[128,1280]{1,0:T(8,128)(2,1)S(1)}, u32[]{:S(2)}, u32[]{:S(2)}) collective-permute-start(bf16[128,1280]{1,0:T(8,128)(2,1)S(1)} %get-tuple-element.76), channel_id=1, source_target_pairs={{0,32},{1,225},{32,64},{33,1},{64,96},{65,33},{96,128},{97,65},{12... | collective-permute-start | bytes 983048 | tf_op jit(solution)/shard_map/ppermute | solution.py:48
  101.7 13.3 %collective-permute-start.18 = (bf16[2,128,1024]{2,1,0:T(8,128)(2,1)S(1)}, bf16[2,128,1024]{2,1,0:T(8,128)(2,1)S(1)}, u32[]{:S(2)}, u32[]{:S(2)}) collective-permute-start(bf16[2,128,1024]{2,1,0:T(8,128)(2,1)S(1)} %add_convert_fusion.4), channel_id=1, source_target_pairs={{0,32},{1,225},{32,64},{33,1},{64,96},{65,33},{96,128},{97,65},{12... | collective-permute-start | bytes 1572872 | tf_op jit(solution)/shard_map/ppermute | solution.py:48
  108.8 13.1 %collective-permute-start.24 = (bf16[2,128,1280]{2,1,0:T(8,128)(2,1)S(1)}, bf16[2,128,1280]{2,1,0:T(8,128)(2,1)S(1)}, u32[]{:S(2)}, u32[]{:S(2)}) collective-permute-start(bf16[2,128,1280]{2,1,0:T(8,128)(2,1)S(1)} %pad_maximum_fusion.6), channel_id=1, source_target_pairs={{0,32},{1,225},{32,64},{33,1},{64,96},{65,33},{96,128},{97,65},{12... | collective-permute-start | bytes 1966088 | tf_op jit(solution)/shard_map/ppermute | solution.py:48
  115.0 13.9 %collective-permute-start.30 = (bf16[2,128,1280]{2,1,0:T(8,128)(2,1)S(1)}, bf16[2,128,1280]{2,1,0:T(8,128)(2,1)S(1)}, u32[]{:S(2)}, u32[]{:S(2)}) collective-permute-start(bf16[2,128,1280]{2,1,0:T(8,128)(2,1)S(1)} %pad_maximum_fusion.7), channel_id=1, source_target_pairs={{0,32},{1,225},{32,64},{33,1},{64,96},{65,33},{96,128},{97,65},{12... | collective-permute-start | bytes 1966088 | tf_op jit(solution)/shard_map/ppermute | solution.py:48
  122.0 13.9 %collective-permute-start.25 = (bf16[2,128,1280]{2,1,0:T(8,128)(2,1)S(1)}, bf16[2,128,1280]{2,1,0:T(8,128)(2,1)S(1)}, u32[]{:S(2)}, u32[]{:S(2)}) collective-permute-start(bf16[2,128,1280]{2,1,0:T(8,128)(2,1)S(1)} %add_convert_fusion.3), channel_id=1, source_target_pairs={{0,32},{1,225},{32,64},{33,1},{64,96},{65,33},{96,128},{97,65},{12... | collective-permute-start | bytes 1966088 | tf_op jit(solution)/shard_map/ppermute | solution.py:48
  135.9 10.3 %collective-permute-start.31 = (bf16[2,128,1280]{2,1,0:T(8,128)(2,1)S(1)}, bf16[2,128,1280]{2,1,0:T(8,128)(2,1)S(1)}, u32[]{:S(2)}, u32[]{:S(2)}) collective-permute-start(bf16[2,128,1280]{2,1,0:T(8,128)(2,1)S(1)} %add_convert_fusion.1), channel_id=1, source_target_pairs={{0,32},{1,225},{32,64},{33,1},{64,96},{65,33},{96,128},{97,65},{12... | collective-permute-start | bytes 1966088 | tf_op jit(solution)/shard_map/ppermute | solution.py:48
  138.9 14.4 %collective-permute-start.26 = (bf16[2,128,1280]{2,1,0:T(8,128)(2,1)S(1)}, bf16[2,128,1280]{2,1,0:T(8,128)(2,1)S(1)}, u32[]{:S(2)}, u32[]{:S(2)}) collective-permute-start(bf16[2,128,1280]{2,1,0:T(8,128)(2,1)S(1)} %add_convert_fusion.2), channel_id=1, source_target_pairs={{0,32},{1,225},{32,64},{33,1},{64,96},{65,33},{96,128},{97,65},{12... | collective-permute-start | bytes 1966088 | tf_op jit(solution)/shard_map/ppermute | solution.py:48
  146.4 13.9 %collective-permute-start.32 = (bf16[2,128,1280]{2,1,0:T(8,128)(2,1)S(1)}, bf16[2,128,1280]{2,1,0:T(8,128)(2,1)S(1)}, u32[]{:S(2)}, u32[]{:S(2)}) collective-permute-start(bf16[2,128,1280]{2,1,0:T(8,128)(2,1)S(1)} %add_convert_fusion), channel_id=1, source_target_pairs={{0,32},{1,225},{32,64},{33,1},{64,96},{65,33},{96,128},{97,65},{12... | collective-permute-start | bytes 1966088 | tf_op jit(solution)/shard_map/ppermute | solution.py:48
  153.3 13.5 %collective-permute-start.27 = (bf16[128,1280]{1,0:T(8,128)(2,1)S(1)}, bf16[128,1280]{1,0:T(8,128)(2,1)S(1)}, u32[]{:S(2)}, u32[]{:S(2)}) collective-permute-start(bf16[128,1280]{1,0:T(8,128)(2,1)S(1)} %slice_bitcast_fusion.4), channel_id=1, source_target_pairs={{0,1},{1,0},{2,3},{3,2},{4,5},{5,4},{6,7},{7,6},{8,9},{9,8},{10,11... | collective-permute-start | bytes 983048 | tf_op jit(solution)/shard_map/ppermute | solution.py:42
  (18 other events, 106.6 us)
